TPU v7x, 32 devices: a whole 2x2x4 slice. The times are simulated.
32 devices in a mesh: grp: 2 (over y), row: 4 (over z), col: 4 (over x, core).
Axes of the slice: x: 2, y: 2, z: 4, core: 2. Of those that a mesh axis runs over, the one named last changes fastest.
Arguments:
- inputs: bfloat16 [256, 16384], P(('grp', 'row'), 'col'), parts along dimension 0, may hold values from -6 to 6
- output_gradient: bfloat16 [256, 16384], P(('grp', 'row'), 'col'), parts along dimension 0, may hold values from -6 to 6
- gate_preactivation: bfloat16 [256, 8192], P('grp', 'row'), parts along dimension 0, may hold values from -6 to 6
- up_preactivation: bfloat16 [256, 8192], P('grp', 'row'), parts along dimension 0, may hold values from -6 to 6
- gate_weight: bfloat16 [16384, 8192], P('col', 'row'), may hold values from -0.046875 to 0.046875
- up_weight: bfloat16 [16384, 8192], P('col', 'row'), may hold values from -0.046875 to 0.046875
- down_weight: bfloat16 [8192, 16384], P('row', 'col'), may hold values from -0.0625 to 0.0625
- up_adapter_entry: bfloat16 [16, 16384], P(None, 'col'), may hold values from -6 to 6
- up_adapter_exit: bfloat16 [16, 8192], P(None, 'row'), may hold values from -0.0032958984 to 0.0032958984
- down_adapter_entry: bfloat16 [16, 8192], P(None, 'row'), may hold values from -6 to 6
- down_adapter_exit: bfloat16 [16, 16384], P(None, 'col'), may hold values from -0.0023956299 to 0.0023956299
- up_adapter_activations: bfloat16 [16, 256], P(None, 'grp'), parts along dimension 1, may hold values from -0.29882812 to 0.29882812
- down_adapter_activations: bfloat16 [16, 256], P(None, 'grp'), parts along dimension 1, may hold values from -0.29882812 to 0.29882812
Outputs:
- grad_inputs: bfloat16 [256, 16384], P(('grp', 'row'), 'col'), parts along dimension 0
- up_entry_gradient: float32 [32, 16384], P('grp', 'col'), parts along dimension 0
- up_exit_gradient: float32 [32, 8192], P('grp', 'row'), parts along dimension 0
- down_entry_gradient: float32 [32, 8192], P('grp', 'row'), parts along dimension 0
- down_exit_gradient: float32 [32, 16384], P('grp', 'col'), parts along dimension 0
There are 2 independent parts, one for each index of `grp`. A program takes and returns all parts, laid end to end along the dimension named above; an argument that names none is the same for every part. Nothing has to cross between parts.
All inputs are finite; a program needn't handle non-finite values.
Results may differ from a plain program's by a relative error of at most 0.005.
Values may be sent and summed in bfloat16 or wider, within the bound.
No kernel may reach another device: no remote copies, remote signals or barrier semaphores. Data moves between devices by JAX's collectives and lax.ppermute only.
A program may use at most 128 MiB of HBM per device.

v0:
```python
import jax
import jax.numpy as jnp
from jax import lax
from jax.sharding import PartitionSpec as P

adapter_scale = 2.0


def contract_trailing(left, right):
    return lax.dot_general(
        left, right, (((1,), (1,)), ((), ())), preferred_element_type=jnp.float32
    )


def contract_leading(left, right, matmul_accuracy=None):
    return lax.dot_general(
        left,
        right,
        (((0,), (0,)), ((), ())),
        precision=matmul_accuracy,
        preferred_element_type=jnp.float32,
    )


def body(
    inputs,
    output_gradient,
    gate_preactivation,
    up_preactivation,
    gate_weight,
    up_weight,
    down_weight,
    up_adapter_entry,
    up_adapter_exit,
    down_adapter_entry,
    down_adapter_exit,
    up_adapter_activations,
    down_adapter_activations,
):
    highest_setting = lax.Precision.HIGHEST
    complete_gradient = lax.all_gather(output_gradient, "row", axis=0, tiled=True)
    down_piece = contract_trailing(complete_gradient, down_adapter_exit)
    hidden_piece = contract_trailing(complete_gradient, down_weight)
    hidden_piece = hidden_piece + adapter_scale * jnp.dot(
        down_piece, down_adapter_entry.astype(jnp.float32), precision=highest_setting
    )
    hidden_gradient, down_full = lax.psum((hidden_piece, down_piece), "col")
    gate_f = gate_preactivation.astype(jnp.float32)
    up_f = up_preactivation.astype(jnp.float32)
    sigmoid_gate = jax.nn.sigmoid(gate_f)
    hidden_state = (gate_f * sigmoid_gate * up_f).astype(jnp.bfloat16)
    gate_grad = (
        hidden_gradient * up_f * sigmoid_gate * (1.0 + gate_f * (1.0 - sigmoid_gate))
    ).astype(jnp.bfloat16)
    up_gradient = (hidden_gradient * gate_f * sigmoid_gate).astype(jnp.bfloat16)
    down_rounded_value = down_full.astype(jnp.bfloat16)
    upper_piece = contract_trailing(up_gradient, up_adapter_exit)
    input_piece = contract_trailing(gate_grad, gate_weight) + contract_trailing(
        up_gradient, up_weight
    )
    input_piece = input_piece + adapter_scale * jnp.dot(
        upper_piece, up_adapter_entry.astype(jnp.float32), precision=highest_setting
    )
    input_grad, upper_full = (
        lax.psum_scatter(input_piece, "row", scatter_dimension=0, tiled=True),
        lax.psum_scatter(upper_piece, "row", scatter_dimension=0, tiled=True),
    )
    up_entry_term = adapter_scale * contract_leading(
        upper_full, inputs.astype(jnp.float32), matmul_accuracy=highest_setting
    )
    up_entry_gradient = lax.psum(up_entry_term, "row")
    up_exit_gradient = adapter_scale * jnp.dot(
        up_adapter_activations, up_gradient, preferred_element_type=jnp.float32
    )
    down_entry_gradient = adapter_scale * contract_leading(down_rounded_value, hidden_state)
    down_exit_gradient = adapter_scale * jnp.dot(
        down_adapter_activations, complete_gradient, preferred_element_type=jnp.float32
    )
    return (
        input_grad.astype(jnp.bfloat16),
        up_entry_gradient,
        up_exit_gradient,
        down_entry_gradient,
        down_exit_gradient,
    )


def solution(mesh):
    placed = (
        P(("grp", "row"), "col"),
        P(("grp", "row"), "col"),
        P("grp", "row"),
        P("grp", "row"),
        P("col", "row"),
        P("col", "row"),
        P("row", "col"),
        P(None, "col"),
        P(None, "row"),
        P(None, "row"),
        P(None, "col"),
        P(None, "grp"),
        P(None, "grp"),
    )
    return jax.shard_map(
        body,
        mesh=mesh,
        in_specs=placed,
        out_specs=(
            P(("grp", "row"), "col"),
            P("grp", "col"),
            P("grp", "row"),
            P("grp", "row"),
            P("grp", "col"),
        ),
        check_vma=False,
    )
```

profile of v0, /device:TPU:0, one launch (start us, length us, event | category | flops | bytes accessed | tf_op | source)
XLA Modules:
  0.0 212.7 jit_solution(2744428697788110122)
XLA Ops:
  7.2 0.0 copy-start
  7.2 0.0 all-gather.2.cloned.1.call-start
  7.3 0.7 all-gather.2.cloned.1.call-update
  8.0 0.0 all-reduce.3.cloned.1.call-start
  8.0 32.3 %all-gather.2.cloned.1.call-done = bf16[128,4096]{1,0:T(8,128)(2,1)} async-done(((bf16[32,4096]{1,0:T(8,128)(2,1)}), bf16[128,4096]{1,0:T(8,128)(2,1)}) %all-gather.2.cloned.1.call-update) | async-done | bytes 1048592 | tf_op jit(solution)/shard_map/all_gather | solution.py:41
  40.3 1.6 fusion.21
  41.9 11.8 %fusion.20 = f32[128,2048]{1,0:T(8,128)S(1)} fusion(bf16[128,4096]{1,0:T(8,128)(2,1)} %all-gather.2.cloned.1.call-done, bf16[2048,4096]{1,0:T(8,128)(2,1)} %param.19), kind=kOutput, calls=%fused_computation.31 | convolution fusion | flops 2147483648 | bytes 18874368 | tf_op jit(solution)/shard_map/dot_general | solution.py:10
  53.7 1.6 fusion.1
  55.3 0.0 all-reduce.3.cloned.1.call-update
  55.3 0.0 reduce-scatter.7.cloned.1.call-start
  55.3 35.7 %all-reduce.3.cloned.1.call-done = f32[128,2048]{1,0:T(8,128)} async-done(((f32[128,2048]{1,0:T(8,128)}), f32[128,2048]{1,0:T(8,128)}) %all-reduce.3.cloned.1.call-update) | async-done | bytes 1048592 | tf_op jit(solution)/shard_map/psum | solution.py:47
  91.0 1.5 fusion.12
  92.5 0.8 copy-done.2
  93.3 0.2 fusion.22
  93.6 0.8 copy.18
  94.3 0.0 reduce-scatter.7.cloned.1.call-update
  94.4 0.2 reduce-scatter.5.cloned.1.call-start
  94.6 13.2 %fusion.13 = f32[128,4096]{1,0:T(8,128)} fusion(bf16[4096,2048]{1,0:T(8,128)(2,1)} %param.17, f32[128,2048]{1,0:T(8,128)} %all-reduce.3.cloned.1.call-done, bf16[128,2048]{1,0:T(8,128)(2,1)S(1)} %copy-done.7, bf16[128,2048]{1,0:T(8,128)(2,1)S(1)} %copy-done.3), kind=kOutput, calls=%fused_computation.26 | convolution fusion | flops 2150629376 | bytes 20971520 | tf_op jit(solution)/shard_map/dot_general | solution.py:10
  107.8 12.3 %convolution_add_fusion = f32[128,4096]{1,0:T(8,128)S(1)} fusion(f32[128,4096]{1,0:T(8,128)} %fusion.13, bf16[128,2048]{1,0:T(8,128)(2,1)} %copy-done.2, bf16[4096,2048]{1,0:T(8,128)(2,1)} %param.18), kind=kOutput, calls=%fused_computation.2 | convolution fusion | flops 2148007936 | bytes 21495808 | tf_op jit(solution)/shard_map/dot_general | solution.py:10
  120.1 2.4 %fusion = f32[128,4096]{1,0:T(8,128)} fusion(f32[128,4096]{1,0:T(8,128)S(1)} %convolution_add_fusion, f32[128,16]{0,1:T(8,128)S(1)} %fusion.22, bf16[16,4096]{1,0:T(8,128)(2,1)S(1)} %copy-done.4), kind=kOutput, calls=%fused_computation.1 | convolution fusion | flops 101711872 | bytes 4333568 | tf_op jit(solution)/shard_map/dot_general | solution.py:61
  122.5 0.0 reduce-scatter.5.cloned.1.call-update
  122.5 0.0 all-reduce.5.cloned.1.call-start
  122.6 6.0 %psum.23 = bf16[128,16]{0,1:T(8,128)(2,1)S(1)} all-reduce(f32[128,16]{0,1:T(8,128)S(1)} %fusion.21), channel_id=1, replica_groups=mesh['grp'=2,'row'=4,'col'=4] {'col'}, use_global_device_ids=true, to_apply=%region_4.0 | all-reduce | flops 2048 | bytes 12288 | tf_op jit(solution)/shard_map/psum | solution.py:47
  128.6 2.4 %convolution_multiply_fusion.5 = f32[16,2048]{1,0:T(8,128)} fusion(bf16[128,2048]{1,0:T(8,128)(2,1)} %param.16, bf16[128,2048]{1,0:T(8,128)(2,1)} %param.15, bf16[128,16]{0,1:T(8,128)(2,1)S(1)} %psum.23), kind=kOutput, calls=%fused_computation.9 | convolution fusion | flops 10518528 | bytes 1183744 | tf_op jit(solution)/shard_map/dot_general | solution.py:16
  131.0 1.7 convolution_multiply_fusion.2
  132.7 0.0 all-reduce.5.cloned.1.call-update
  132.8 1.6 convolution_multiply_fusion.1
  134.4 1.9 fusion.2
  136.3 30.6 %reduce-scatter.5.cloned.1.call-done = f32[32,4096]{1,0:T(8,128)} async-done(((f32[128,4096]{1,0:T(8,128)}), f32[32,4096]{1,0:T(8,128)}) %reduce-scatter.5.cloned.1.call-update) | async-done | bytes 524304 | tf_op jit(solution)/shard_map/reduce_scatter | solution.py:65
  166.9 1.8 convert_element_type.28
  168.7 35.8 %all-reduce.5.cloned.1.call-done = f32[16,4096]{1,0:T(8,128)} async-done(((f32[16,4096]{1,0:T(8,128)}), f32[16,4096]{1,0:T(8,128)}) %all-reduce.5.cloned.1.call-update) | async-done | bytes 262160 | tf_op jit(solution)/shard_map/psum | solution.py:71
  204.5 1.7 copy.22
  (15 shorter events, 0.0 us)
Async XLA Ops:
  7.2 123.8 %copy-start = (bf16[32,4096]{1,0:T(8,128)(2,1)S(1)}, bf16[32,4096]{1,0:T(8,128)(2,1)}, u32[]{:S(2)}) copy-start(bf16[32,4096]{1,0:T(8,128)(2,1)} %param.13) | copy-start | bytes 786436
  7.2 46.5 %copy-start.5 = (bf16[16,2048]{1,0:T(8,128)(2,1)S(1)}, bf16[16,2048]{1,0:T(8,128)(2,1)}, u32[]{:S(2)}) copy-start(bf16[16,2048]{1,0:T(8,128)(2,1)} %param.22) | copy-start | bytes 196612
  7.2 83.8 %copy-start.3 = (bf16[128,2048]{1,0:T(8,128)(2,1)S(1)}, bf16[128,2048]{1,0:T(8,128)(2,1)}, u32[]{:S(2)}) copy-start(bf16[128,2048]{1,0:T(8,128)(2,1)} %param.15) | copy-start | bytes 1572868
  7.2 86.1 %copy-start.6 = (bf16[16,2048]{1,0:T(8,128)(2,1)S(1)}, bf16[16,2048]{1,0:T(8,128)(2,1)}, u32[]{:S(2)}) copy-start(bf16[16,2048]{1,0:T(8,128)(2,1)} %param.21) | copy-start | bytes 196612
  7.2 87.4 %copy-start.7 = (bf16[128,2048]{1,0:T(8,128)(2,1)S(1)}, bf16[128,2048]{1,0:T(8,128)(2,1)}, u32[]{:S(2)}) copy-start(bf16[128,2048]{1,0:T(8,128)(2,1)} %param.16) | copy-start | bytes 1572868
  7.2 33.1 %all-gather.2.cloned.1.call-start = ((), (), s32[]{:S(2)}) async-start(), calls=%async_computation.2 | async-start | bytes 1310720 | tf_op jit(solution)/shard_map/all_gather | solution.py:41
  8.0 83.1 %all-reduce.3.cloned.1.call-start = ((), (), s32[]{:S(2)}) async-start(), calls=%async_computation.3 | async-start | bytes 2097152 | tf_op jit(solution)/shard_map/psum | solution.py:47
  55.3 75.7 %reduce-scatter.7.cloned.1.call-start = ((), (), s32[]{:S(2)}) async-start(), calls=%async_computation.6 | async-start | bytes 81920
  92.5 0.8 copy-start.2
  94.4 25.7 %copy-start.4 = (bf16[16,4096]{1,0:T(8,128)(2,1)S(1)}, bf16[16,4096]{1,0:T(8,128)(2,1)}, u32[]{:S(2)}) copy-start(bf16[16,4096]{1,0:T(8,128)(2,1)} %param.20) | copy-start | bytes 393220
  94.4 72.5 %reduce-scatter.5.cloned.1.call-start = ((), (), s32[]{:S(2)}) async-start(), calls=%async_computation.4 | async-start | bytes 2621440 | tf_op jit(solution)/shard_map/reduce_scatter | solution.py:65
  107.8 25.0 %copy-start.1 = (bf16[128,4096]{1,0:T(8,128)(2,1)S(1)}, bf16[128,4096]{1,0:T(8,128)(2,1)}, u32[]{:S(2)}) copy-start(bf16[128,4096]{1,0:T(8,128)(2,1)} %all-gather.2.cloned.1.call-done) | copy-start | bytes 3145732
  122.5 82.0 %all-reduce.5.cloned.1.call-start = ((), (), s32[]{:S(2)}) async-start(), calls=%async_computation.5 | async-start | bytes 524288 | tf_op jit(solution)/shard_map/psum | solution.py:71
Sparse Core Ops, SparseCore 0:
  9.6 30.6 all-gather.1
  55.4 35.5 all-reduce.2
  94.5 19.4 reduce-scatter.6
  122.6 44.2 reduce-scatter.4
  169.8 34.6 all-reduce.4
where the time goes:
time: 213 us
  waiting for transfers between devices  135 us (63%)
  matrix products  50.8 us (24%)
  between operations  13.9 us (7%)
  blocking collectives  6 us (3%)
  other arithmetic  3.28 us (2%)
  local copies, waits for them, and re-layouts  3.27 us (2%)
    dot_general x5, matrix products, contract_trailing(): lax.dot_general(left, right, (((1,), (1,)), ((), ())), preferred_element_...  39 us
    psum x1, waiting for transfers between devices, body(): up_entry_gradient = lax.psum(up_entry_term, 'row')  35.8 us
    psum x1, waiting for transfers between devices, body(): hidden_gradient, down_full = lax.psum((hidden_piece, down_piece), 'col')  35.7 us
    all_gather x1, waiting for transfers between devices, body(): lax.all_gather(output_gradient, 'row', axis=0, tiled=True)  32.3 us
    reduce_scatter x1, waiting for transfers between devices, body(): lax.psum_scatter(input_piece, 'row', scatter_dimension=0, tiled=True)  30.6 us
    psum x1, blocking collectives, body(): hidden_gradient, down_full = lax.psum((hidden_piece, down_piece), 'col')  6 us
  transfers between devices with their start and end apart: 5, of which 4 were waited for; matrix products, arithmetic and copies ran while one was open for 18% of the time, Pallas kernels for 0%

commit v1 on v0

--- a/solution.py
+++ b/solution.py
@@ -68,7 +68,11 @@
     up_entry_term = adapter_scale * contract_leading(
         upper_full, inputs.astype(jnp.float32), matmul_accuracy=highest_setting
     )
-    up_entry_gradient = lax.psum(up_entry_term, "row")
+    up_entry_gradient = up_entry_term
+    for hop in (1, 2):
+        up_entry_gradient = up_entry_gradient + lax.ppermute(
+            up_entry_gradient, "row", [(dev, dev ^ hop) for dev in range(4)]
+        )
     up_exit_gradient = adapter_scale * jnp.dot(
         up_adapter_activations, up_gradient, preferred_element_type=jnp.float32
     )

time: 213 us -> 188 us (0.88)
  waiting for transfers between devices: 135 us -> 110 us
    ppermute x0 -> x2, waiting for transfers between devices: none -> 41.5 us  [body(): lax.ppermute(up_entry_gradient, 'row', [(dev, dev ^ hop) for dev in range...]
    psum x1 -> x0, waiting for transfers between devices: 35.8 us -> none  [body(): up_entry_gradient = lax.psum(up_entry_term, 'row')]
    reduce_scatter x1, waiting for transfers between devices: 30.6 us -> 0.01 us  [body(): lax.psum_scatter(input_piece, 'row', scatter_dimension=0, tiled=True)]
  transfers between devices with their start and end apart: 5 -> 6, of which waited for: 4 -> 4; matrix products, arithmetic and copies ran while one was open for 18% -> 19% of each run, Pallas kernels for 0% -> 0%
where the time goes in v1:
time: 188 us
  waiting for transfers between devices  110 us (59%)
  matrix products  49.9 us (27%)
  between operations  13.9 us (7%)
  blocking collectives  6 us (3%)
  other arithmetic  4.04 us (2%)
  starting transfers between devices  2.26 us (1%)
    ppermute x2, waiting for transfers between devices, body(): lax.ppermute(up_entry_gradient, 'row', [(dev, dev ^ hop) for dev in range...  41.5 us
    dot_general x5, matrix products, contract_trailing(): lax.dot_general(left, right, (((1,), (1,)), ((), ())), preferred_element_...  39 us
    psum x1, waiting for transfers between devices, body(): hidden_gradient, down_full = lax.psum((hidden_piece, down_piece), 'col')  35.7 us
    all_gather x1, waiting for transfers between devices, body(): lax.all_gather(output_gradient, 'row', axis=0, tiled=True)  32.3 us
    psum x1, blocking collectives, body(): hidden_gradient, down_full = lax.psum((hidden_piece, down_piece), 'col')  6 us
  transfers between devices with their start and end apart: 6, of which 4 were waited for; matrix products, arithmetic and copies ran while one was open for 19% of the time, Pallas kernels for 0%

profile of v1, /device:TPU:0, one launch (start us, length us, event | category | flops | bytes accessed | tf_op | source)
XLA Modules:
  0.0 187.9 jit_solution(1550529962076423907)
XLA Ops:
  7.2 0.0 all-gather.2.cloned.1.call-start
  7.3 0.7 all-gather.2.cloned.1.call-update
  8.0 0.0 all-reduce.2.cloned.1.call-start
  8.0 32.3 %all-gather.2.cloned.1.call-done = bf16[128,4096]{1,0:T(8,128)(2,1)} async-done(((bf16[32,4096]{1,0:T(8,128)(2,1)}), bf16[128,4096]{1,0:T(8,128)(2,1)}) %all-gather.2.cloned.1.call-update) | async-done | bytes 1048592 | tf_op jit(solution)/shard_map/all_gather | solution.py:41
  40.3 1.6 fusion.21
  41.9 11.8 %fusion.20 = f32[128,2048]{1,0:T(8,128)S(1)} fusion(bf16[128,4096]{1,0:T(8,128)(2,1)} %all-gather.2.cloned.1.call-done, bf16[2048,4096]{1,0:T(8,128)(2,1)} %param.19), kind=kOutput, calls=%fused_computation.31 | convolution fusion | flops 2147483648 | bytes 18874368 | tf_op jit(solution)/shard_map/dot_general | solution.py:10
  53.7 1.6 fusion.1
  55.3 0.0 all-reduce.2.cloned.1.call-update
  55.3 0.0 reduce-scatter.7.cloned.1.call-start
  55.3 35.7 %all-reduce.2.cloned.1.call-done = f32[128,2048]{1,0:T(8,128)} async-done(((f32[128,2048]{1,0:T(8,128)}), f32[128,2048]{1,0:T(8,128)}) %all-reduce.2.cloned.1.call-update) | async-done | bytes 1048592 | tf_op jit(solution)/shard_map/psum | solution.py:47
  91.0 1.5 fusion.12
  92.5 0.8 copy-done.2
  93.3 0.2 fusion.22
  93.6 0.8 copy.18
  94.3 0.0 reduce-scatter.7.cloned.1.call-update
  94.4 0.2 reduce-scatter.5.cloned.1.call-start
  94.6 13.2 %fusion.13 = f32[128,4096]{1,0:T(8,128)} fusion(bf16[4096,2048]{1,0:T(8,128)(2,1)} %param.17, f32[128,2048]{1,0:T(8,128)} %all-reduce.2.cloned.1.call-done, bf16[128,2048]{1,0:T(8,128)(2,1)S(1)} %copy-done.7, bf16[128,2048]{1,0:T(8,128)(2,1)S(1)} %copy-done.3), kind=kOutput, calls=%fused_computation.26 | convolution fusion | flops 2150629376 | bytes 20971520 | tf_op jit(solution)/shard_map/dot_general | solution.py:10
  107.8 12.3 %convolution_add_fusion = f32[128,4096]{1,0:T(8,128)S(1)} fusion(f32[128,4096]{1,0:T(8,128)} %fusion.13, bf16[128,2048]{1,0:T(8,128)(2,1)} %copy-done.2, bf16[4096,2048]{1,0:T(8,128)(2,1)} %param.18), kind=kOutput, calls=%fused_computation.2 | convolution fusion | flops 2148007936 | bytes 21495808 | tf_op jit(solution)/shard_map/dot_general | solution.py:10
  120.1 2.4 %fusion = f32[128,4096]{1,0:T(8,128)} fusion(f32[128,4096]{1,0:T(8,128)S(1)} %convolution_add_fusion, f32[128,16]{0,1:T(8,128)S(1)} %fusion.22, bf16[16,4096]{1,0:T(8,128)(2,1)S(1)} %copy-done.4), kind=kOutput, calls=%fused_computation.1 | convolution fusion | flops 101711872 | bytes 4333568 | tf_op jit(solution)/shard_map/dot_general | solution.py:61
  122.5 0.0 reduce-scatter.5.cloned.1.call-update
  122.5 6.0 %psum.15 = bf16[128,16]{0,1:T(8,128)(2,1)S(1)} all-reduce(f32[128,16]{0,1:T(8,128)S(1)} %fusion.21), channel_id=1, replica_groups=mesh['grp'=2,'row'=4,'col'=4] {'col'}, use_global_device_ids=true, to_apply=%region_3.0 | all-reduce | flops 2048 | bytes 12288 | tf_op jit(solution)/shard_map/psum | solution.py:47
  128.5 0.0 reduce-scatter.7.cloned.1.call-done
  128.5 1.0 convolution_multiply_fusion.2
  129.6 1.6 collective-permute-start
  131.1 2.3 %convolution_multiply_fusion.5 = f32[16,2048]{1,0:T(8,128)} fusion(bf16[128,2048]{1,0:T(8,128)(2,1)} %param.16, bf16[128,2048]{1,0:T(8,128)(2,1)} %param.15, bf16[128,16]{0,1:T(8,128)(2,1)S(1)} %psum.15), kind=kOutput, calls=%fused_computation.9 | convolution fusion | flops 10518528 | bytes 1183744 | tf_op jit(solution)/shard_map/dot_general | solution.py:16
  133.4 15.9 %collective-permute-done = f32[16,4096]{1,0:T(8,128)S(1)} collective-permute-done((f32[16,4096]{1,0:T(8,128)S(1)}, f32[16,4096]{1,0:T(8,128)S(1)}, u32[]{:S(2)}, u32[]{:S(2)}) %collective-permute-start) | collective-permute-done | bytes 262176 | tf_op jit(solution)/shard_map/ppermute | solution.py:73
  149.3 0.4 collective-permute-start.1
  149.7 1.6 convolution_multiply_fusion.1
  151.3 1.9 %fusion.2 = f32[16,2048]{1,0:T(8,128)} fusion(bf16[16,128]{1,0:T(8,128)(2,1)} %param.24, bf16[128,2048]{1,0:T(8,128)(2,1)} %copy-done.2), kind=kOutput, calls=%fused_computation.8 | convolution fusion | flops 8421376 | bytes 659456 | tf_op jit(solution)/shard_map/dot_general | solution.py:76
  153.2 25.6 %collective-permute-done.1 = f32[16,4096]{1,0:T(8,128)S(1)} collective-permute-done((f32[16,4096]{1,0:T(8,128)S(1)}, f32[16,4096]{1,0:T(8,128)S(1)}, u32[]{:S(2)}, u32[]{:S(2)}) %collective-permute-start.1) | collective-permute-done | bytes 262176 | tf_op jit(solution)/shard_map/ppermute | solution.py:73
  178.9 0.7 add.35
  179.6 1.8 convert_element_type.28
  (17 shorter events, 0.1 us)
Async XLA Ops:
  7.2 121.4 %copy-start = (bf16[32,4096]{1,0:T(8,128)(2,1)S(1)}, bf16[32,4096]{1,0:T(8,128)(2,1)}, u32[]{:S(2)}) copy-start(bf16[32,4096]{1,0:T(8,128)(2,1)} %param.13) | copy-start | bytes 786436
  7.2 46.5 %copy-start.5 = (bf16[16,2048]{1,0:T(8,128)(2,1)S(1)}, bf16[16,2048]{1,0:T(8,128)(2,1)}, u32[]{:S(2)}) copy-start(bf16[16,2048]{1,0:T(8,128)(2,1)} %param.22) | copy-start | bytes 196612
  7.2 83.8 %copy-start.3 = (bf16[128,2048]{1,0:T(8,128)(2,1)S(1)}, bf16[128,2048]{1,0:T(8,128)(2,1)}, u32[]{:S(2)}) copy-start(bf16[128,2048]{1,0:T(8,128)(2,1)} %param.15) | copy-start | bytes 1572868
  7.2 86.1 %copy-start.6 = (bf16[16,2048]{1,0:T(8,128)(2,1)S(1)}, bf16[16,2048]{1,0:T(8,128)(2,1)}, u32[]{:S(2)}) copy-start(bf16[16,2048]{1,0:T(8,128)(2,1)} %param.21) | copy-start | bytes 196612
  7.2 87.4 %copy-start.7 = (bf16[128,2048]{1,0:T(8,128)(2,1)S(1)}, bf16[128,2048]{1,0:T(8,128)(2,1)}, u32[]{:S(2)}) copy-start(bf16[128,2048]{1,0:T(8,128)(2,1)} %param.16) | copy-start | bytes 1572868
  7.2 33.1 %all-gather.2.cloned.1.call-start = ((), (), s32[]{:S(2)}) async-start(), calls=%async_computation.2 | async-start | bytes 1310720 | tf_op jit(solution)/shard_map/all_gather | solution.py:41
  8.0 83.1 %all-reduce.2.cloned.1.call-start = ((), (), s32[]{:S(2)}) async-start(), calls=%async_computation.3 | async-start | bytes 2097152 | tf_op jit(solution)/shard_map/psum | solution.py:47
  55.3 73.2 %reduce-scatter.7.cloned.1.call-start = ((), (), s32[]{:S(2)}) async-start(), calls=%async_computation.5 | async-start | bytes 81920
  92.5 0.8 copy-start.2
  94.4 25.7 %copy-start.4 = (bf16[16,4096]{1,0:T(8,128)(2,1)S(1)}, bf16[16,4096]{1,0:T(8,128)(2,1)}, u32[]{:S(2)}) copy-start(bf16[16,4096]{1,0:T(8,128)(2,1)} %param.20) | copy-start | bytes 393220
  94.4 85.2 %reduce-scatter.5.cloned.1.call-start = ((), (), s32[]{:S(2)}) async-start(), calls=%async_computation.4 | async-start | bytes 2621440 | tf_op jit(solution)/shard_map/reduce_scatter | solution.py:65
  107.8 41.9 %copy-start.1 = (bf16[128,4096]{1,0:T(8,128)(2,1)S(1)}, bf16[128,4096]{1,0:T(8,128)(2,1)}, u32[]{:S(2)}) copy-start(bf16[128,4096]{1,0:T(8,128)(2,1)} %all-gather.2.cloned.1.call-done) | copy-start | bytes 3145732
  129.6 19.7 %collective-permute-start = (f32[16,4096]{1,0:T(8,128)S(1)}, f32[16,4096]{1,0:T(8,128)S(1)}, u32[]{:S(2)}, u32[]{:S(2)}) collective-permute-start(f32[16,4096]{1,0:T(8,128)S(1)} %convolution_multiply_fusion.2), channel_id=1, source_target_pairs={{0,4},{4,0},{8,12},{12,8},{1,5},{5,1},{9,13},{13,9},{2,6},{6,2},{1... | collective-permute-start | bytes 786440 | tf_op jit(solution)/shard_map/ppermute | solution.py:73
  149.3 29.5 %collective-permute-start.1 = (f32[16,4096]{1,0:T(8,128)S(1)}, f32[16,4096]{1,0:T(8,128)S(1)}, u32[]{:S(2)}, u32[]{:S(2)}) collective-permute-start(f32[16,4096]{1,0:T(8,128)S(1)} %add.34), channel_id=1, source_target_pairs={{0,8},{4,12},{8,0},{12,4},{1,9},{5,13},{9,1},{13,5},{2,10},{6,14},... | collective-permute-start | bytes 786440 | tf_op jit(solution)/shard_map/ppermute | solution.py:73
Sparse Core Ops, SparseCore 0:
  9.6 30.6 all-gather.1
  55.4 35.5 all-reduce.1
  94.5 19.4 reduce-scatter.6
  122.6 55.2 reduce-scatter.4
